TPU v7x, 32 devices: a whole 2x2x4 slice. The times are simulated.
32 devices in a mesh: gx: 4 (over y, core), gy: 8 (over z, x).
Axes of the slice: x: 2, y: 2, z: 4, core: 2. Of those that a mesh axis runs over, the one named last changes fastest.
Arguments:
- columns: float32 [16384, 512], P(('gx', 'gy')), may hold values from -6 to 6
- col_basis: float32 [16384, 128], P(('gx', 'gy')), may hold values from -0.25 to 0.25
- row_basis: float32 [16384, 128], P(('gx', 'gy')), may hold values from -0.5 to 0.5
- order_perm: int32 [32, 512], P(('gx', 'gy')), may hold values from 0 to 511, each once within a row
- near_blocks: float32 [128, 5, 128, 128], P(('gx', 'gy')), may hold values from -0.25 to 0.25
- band_offsets: int32 [128, 5], P(('gx', 'gy')), may hold values from -4 to 4
- transfer: float32 [4, 2, 128, 128], replicated, may hold values from -0.375 to 0.375
- coupling: float32 [5, 128, 128], replicated, may hold values from -0.5 to 0.5
Outputs:
- product: float32 [16384, 512], P(('gx', 'gy'))
Inputs may be any that keep to these rules, and one draw needn't show every extreme that they name: `order_perm`: each row is a permutation of the 512 rows of its leaf.
All inputs are finite; a program needn't handle non-finite values.
Results may differ from a plain program's by a relative error of at most 0.0001.
Values sent between devices are 32-bit elements; how exact they have to be, the bound alone decides.
No kernel may reach another device: no remote copies, remote signals or barrier semaphores. Data moves between devices by JAX's collectives and lax.ppermute only.
A program may use at most 64 MiB of HBM per device.

v0:
```python
import jax
import jax.numpy as jnp
from jax import lax
from jax.sharding import PartitionSpec as P

BLK = 128
REACH = 4


def from_partner(x, axis, bit):
    return lax.ppermute(x, axis, [(i, i ^ 1 << bit) for i in range(lax.axis_size(axis))])


def extended(x, sides, width):
    for axis, dim in sides:
        size, length = (lax.axis_size(axis), x.shape[dim])
        up = [(i, (i + 1) % size) for i in range(size - 1)]
        down = [(j, i) for i, j in up]
        last = lax.slice_in_dim(x, length - width, length, axis=dim)
        initial = lax.slice_in_dim(x, 0, width, axis=dim)
        before = lax.ppermute(last, axis, up)
        after = lax.ppermute(initial, axis, down)
        x = jnp.concatenate([before, x, after], axis=dim)
    return x


def near_field(padded_rows, blocks_here, offsets_here):
    rhs_cols = padded_rows.shape[1]
    column_blocks = padded_rows.reshape(-1, BLK, rhs_cols)
    block_index = jnp.arange(offsets_here.shape[0], dtype=jnp.int32)[:, None] + offsets_here + REACH
    taken = column_blocks[block_index]
    result = jnp.einsum("jbrc,jbcn->jrn", blocks_here, taken, precision=lax.Precision.HIGHEST)
    return result.reshape(-1, rhs_cols)


def sibling_step(own_node, sibling, which_side, transfer, coupling, level, levels):
    exact = lax.Precision.HIGHEST
    on_left = which_side == 0
    left_node = jnp.where(on_left, own_node, sibling)
    right_node = jnp.where(on_left, sibling, own_node)
    chosen = jnp.where(on_left, coupling[level], coupling[level].T)
    coupled = jnp.dot(chosen, sibling, precision=exact)
    if level < levels - 1:
        parent = jnp.dot(transfer[level, 0].T, left_node, precision=exact) + jnp.dot(
            transfer[level, 1].T, right_node, precision=exact
        )
    else:
        parent = own_node
    return (coupled, parent)


def per_device(
    columns, col_basis, row_basis, order_perm, near_blocks, band_offsets, transfer, coupling
):
    exact = lax.Precision.HIGHEST
    across = lax.axis_size("gx")
    along = lax.axis_size("gy")
    high_bits = across.bit_length() - 1
    low_bits = along.bit_length() - 1
    levels = high_bits + low_bits
    index_x = lax.axis_index("gx")
    index_y = lax.axis_index("gy")
    leaf_index = index_x * along + index_y
    tree_cols = columns[order_perm[0]]
    skeleton = lax.dot_general(col_basis, tree_cols, (((0,), (0,)), ((), ())), precision=exact)
    couples = []
    for level in range(low_bits):
        sibling = from_partner(skeleton, "gy", level)
        which_side = index_y >> level & 1
        coupled, skeleton = sibling_step(
            skeleton, sibling, which_side, transfer, coupling, level, levels
        )
        couples.append(coupled)
    for bit_number in range(high_bits):
        level = low_bits + bit_number
        sibling = from_partner(skeleton, "gx", bit_number)
        which_side = index_x >> bit_number & 1
        coupled, skeleton = sibling_step(
            skeleton, sibling, which_side, transfer, coupling, level, levels
        )
        couples.append(coupled)
    expand = couples[levels - 1]
    for level in range(levels - 2, -1, -1):
        which_side = leaf_index >> level & 1
        chosen = jnp.where(which_side == 0, transfer[level, 0], transfer[level, 1])
        expand = couples[level] + jnp.dot(chosen, expand, precision=exact)
    far = jnp.dot(row_basis, expand, precision=exact)
    padded = extended(tree_cols, ((("gx", "gy"), 0),), REACH * BLK)
    near = near_field(padded, near_blocks, band_offsets)
    tree_out = near + far
    return jnp.zeros_like(tree_out).at[order_perm[0]].set(tree_out)


def solution(mesh):
    placed = (
        P(("gx", "gy"), None),
        P(("gx", "gy"), None),
        P(("gx", "gy"), None),
        P(("gx", "gy"), None),
        P(("gx", "gy"), None, None, None),
        P(("gx", "gy"), None),
        P(),
        P(),
    )
    return jax.shard_map(
        per_device, mesh=mesh, in_specs=placed, out_specs=P(("gx", "gy"), None), check_vma=False
    )
```

profile of v0, /device:TPU:0, one launch (start us, length us, event | category | flops | bytes accessed | tf_op | source)
XLA Modules:
  0.0 110.4 jit_solution(4050834841259023983)
XLA Ops:
  0.8 3.3 %gather_fusion = f32[512,512]{1,0:T(8,128)S(1)} fusion(f32[512,512]{1,0:T(8,128)} %param.8, s32[1024]{0:T(1024)S(1)} %pad_clamp_fusion.1), kind=kCustom, calls=%fused_computation | custom fusion | bytes 2099200 | tf_op jit(solution)/shard_map/gather | solution.py:64
  4.1 1.8 %convolution_bitcast_fusion.1 = f32[128,512]{0,1:T(8,128)S(1)} fusion(f32[512,512]{1,0:T(8,128)S(1)} %gather_fusion, f32[512,128]{1,0:T(8,128)S(1)} %copy-done.8), kind=kOutput, calls=%fused_computation.18 | convolution fusion | flops 402653184 | bytes 1572864 | tf_op jit(solution)/shard_map/dot_general | solution.py:65
  5.9 3.0 %collective-permute-start.2 = (f32[128,512]{0,1:T(8,128)S(1)}, f32[128,512]{0,1:T(8,128)S(1)}, u32[]{:S(2)}, u32[]{:S(2)}) collective-permute-start(f32[128,512]{0,1:T(8,128)S(1)} %convolution_bitcast_fusion.1), channel_id=1, source_target_pairs={{0,1},{1,0},{2,3},{3,2},{4,5},{5,4},{6,7},{7,6},{8,9},{9,8},{10,11... | collective-permute-start | bytes 786440 | tf_op jit(solution)/shard_map/ppermute | solution.py:11
  9.0 6.3 %collective-permute-done.2 = f32[128,512]{0,1:T(8,128)S(1)} collective-permute-done((f32[128,512]{0,1:T(8,128)S(1)}, f32[128,512]{0,1:T(8,128)S(1)}, u32[]{:S(2)}, u32[]{:S(2)}) %collective-permute-start.2) | collective-permute-done | bytes 262176 | tf_op jit(solution)/shard_map/ppermute | solution.py:11
  15.3 1.2 %fusion.16 = f32[512,128]{1,0:T(8,128)S(1)} fusion(f32[128,512]{0,1:T(8,128)S(1)} %collective-permute-done.2, f32[128,512]{0,1:T(8,128)S(1)} %convolution_bitcast_fusion.1, pred[]{:T(512)S(6)} %eq.27, f32[4,2,128,128]{3,2,1,0:T(8,128)} %param.14), kind=kOutput, calls=%fused_computation.30 | convolution fusion | flops 100728832 | bytes 851969 | tf_op jit(solution)/shard_map/dot_general | solution.py:44
  17.8 1.9 %collective-permute-start.3 = (f32[128,512]{0,1:T(8,128)S(1)}, f32[128,512]{0,1:T(8,128)S(1)}, u32[]{:S(2)}, u32[]{:S(2)}) collective-permute-start(f32[128,512]{0,1:T(8,128)S(1)} %fusion.4), channel_id=1, source_target_pairs={{0,2},{1,3},{2,0},{3,1},{4,6},{5,7},{6,4},{7,5},{8,10},{9,11},{10,... | collective-permute-start | bytes 786440 | tf_op jit(solution)/shard_map/ppermute | solution.py:11
  19.6 5.6 %collective-permute-done.3 = f32[128,512]{0,1:T(8,128)S(1)} collective-permute-done((f32[128,512]{0,1:T(8,128)S(1)}, f32[128,512]{0,1:T(8,128)S(1)}, u32[]{:S(2)}, u32[]{:S(2)}) %collective-permute-start.3) | collective-permute-done | bytes 262176 | tf_op jit(solution)/shard_map/ppermute | solution.py:11
  25.3 1.2 %fusion.13 = f32[512,128]{1,0:T(8,128)S(1)} fusion(f32[128,512]{0,1:T(8,128)S(1)} %collective-permute-done.3, f32[128,512]{0,1:T(8,128)S(1)} %fusion.4, pred[]{:T(512)S(6)} %eq.29, f32[4,2,128,128]{3,2,1,0:T(8,128)} %param.14), kind=kOutput, calls=%fused_computation.27 | convolution fusion | flops 100728832 | bytes 851969 | tf_op jit(solution)/shard_map/dot_general | solution.py:44
  27.8 2.6 %collective-permute-start.4 = (f32[128,512]{0,1:T(8,128)S(1)}, f32[128,512]{0,1:T(8,128)S(1)}, u32[]{:S(2)}, u32[]{:S(2)}) collective-permute-start(f32[128,512]{0,1:T(8,128)S(1)} %fusion.3), channel_id=1, source_target_pairs={{0,4},{1,5},{2,6},{3,7},{4,0},{5,1},{6,2},{7,3},{8,12},{9,13},{10,... | collective-permute-start | bytes 786440 | tf_op jit(solution)/shard_map/ppermute | solution.py:11
  30.4 1.3 %collective-permute-start.1 = (f32[512,512]{1,0:T(8,128)S(1)}, f32[512,512]{1,0:T(8,128)}, u32[]{:S(2)}, u32[]{:S(2)}) collective-permute-start(f32[512,512]{1,0:T(8,128)S(1)} %gather_fusion), channel_id=1, source_target_pairs={{1,0},{2,1},{3,2},{4,3},{5,4},{6,5},{7,6},{8,7},{9,8},{10,9},{11,1... | collective-permute-start | bytes 3145736 | tf_op jit(solution)/shard_map/ppermute | solution.py:22
  31.7 5.5 %collective-permute-start = (f32[512,512]{1,0:T(8,128)S(1)}, f32[512,512]{1,0:T(8,128)}, u32[]{:S(2)}, u32[]{:S(2)}) collective-permute-start(f32[512,512]{1,0:T(8,128)S(1)} %gather_fusion), channel_id=1, source_target_pairs={{0,1},{1,2},{2,3},{3,4},{4,5},{5,6},{6,7},{7,8},{8,9},{9,10},{10,1... | collective-permute-start | bytes 3145736 | tf_op jit(solution)/shard_map/ppermute | solution.py:21
  37.3 4.5 %collective-permute-done.4 = f32[128,512]{0,1:T(8,128)S(1)} collective-permute-done((f32[128,512]{0,1:T(8,128)S(1)}, f32[128,512]{0,1:T(8,128)S(1)}, u32[]{:S(2)}, u32[]{:S(2)}) %collective-permute-start.4) | collective-permute-done | bytes 262176 | tf_op jit(solution)/shard_map/ppermute | solution.py:11
  41.8 1.2 %fusion.10 = f32[512,128]{1,0:T(8,128)S(1)} fusion(f32[128,512]{0,1:T(8,128)S(1)} %collective-permute-done.4, f32[128,512]{0,1:T(8,128)S(1)} %fusion.3, pred[]{:T(512)S(6)} %eq.31, f32[4,2,128,128]{3,2,1,0:T(8,128)} %param.14), kind=kOutput, calls=%fused_computation.24 | convolution fusion | flops 100728832 | bytes 851969 | tf_op jit(solution)/shard_map/dot_general | solution.py:44
  43.1 1.9 %fusion.2 = f32[128,512]{0,1:T(8,128)} fusion(f32[512,128]{1,0:T(8,128)S(1)} %fusion.10, f32[128,512]{0,1:T(8,128)S(1)} %fusion.3, f32[128,512]{0,1:T(8,128)S(1)} %collective-permute-done.4, pred[]{:T(512)S(6)} %eq.31, f32[4,2,128,128]{3,2,1,0:T(8,128)} %param.14), kind=kOutput, calls=%fused_computation.10 | convolution fusion | flops 100794368 | bytes 1114113 | tf_op jit(solution)/shard_map/dot_general | solution.py:44
  45.0 1.7 %slice_bitcast_fusion.4 = (f32[128,128]{1,0:T(8,128)}, f32[128,128]{1,0:T(8,128)S(1)}, f32[128,128]{1,0:T(8,128)}, f32[128,128]{1,0:T(8,128)}, f32[128,128]{1,0:T(8,128)}) fusion(f32[5,128,128]{2,1,0:T(8,128)} %param.15), kind=kLoop, calls=%fused_computation.71 | loop fusion | bytes 655360 | tf_op jit(solution)/shard_map/squeeze | solution.py:41
  49.3 1.6 %copy.19 = f32[128,128]{0,1:T(8,128)} copy(f32[128,128]{1,0:T(8,128)} %get-tuple-element.8) | data formatting | bytes 131072 | tf_op jit(solution)/shard_map/squeeze | solution.py:41
  50.8 1.6 %copy.18 = f32[128,128]{0,1:T(8,128)} copy(f32[128,128]{1,0:T(8,128)} %get-tuple-element.9) | data formatting | bytes 131072 | tf_op jit(solution)/shard_map/squeeze | solution.py:41
  52.4 1.3 %fusion.7 = f32[512,128]{1,0:T(8,128)S(1)} fusion(f32[128,512]{0,1:T(8,128)S(1)} %collective-permute-done.5, f32[128,512]{0,1:T(8,128)} %fusion.2, pred[]{:T(512)S(6)} %eq.33, f32[4,2,128,128]{3,2,1,0:T(8,128)} %param.14), kind=kOutput, calls=%fused_computation.21 | convolution fusion | flops 100728832 | bytes 851969 | tf_op jit(solution)/shard_map/dot_general | solution.py:44
  53.7 2.0 %fusion.1 = f32[128,512]{0,1:T(8,128)} fusion(f32[512,128]{1,0:T(8,128)S(1)} %fusion.7, f32[128,512]{0,1:T(8,128)} %fusion.2, f32[128,512]{0,1:T(8,128)S(1)} %collective-permute-done.5, pred[]{:T(512)S(6)} %eq.33, f32[4,2,128,128]{3,2,1,0:T(8,128)} %param.14), kind=kOutput, calls=%fused_computation.7 | convolution fusion | flops 100794368 | bytes 1114113 | tf_op jit(solution)/shard_map/dot_general | solution.py:44
  55.8 1.5 %collective-permute-start.6 = (f32[128,512]{0,1:T(8,128)}, f32[128,512]{0,1:T(8,128)}, u32[]{:S(2)}, u32[]{:S(2)}) collective-permute-start(f32[128,512]{0,1:T(8,128)} %fusion.1), channel_id=1, source_target_pairs={{0,16},{8,24},{16,0},{24,8},{1,17},{9,25},{17,1},{25,9},{2,18},{10... | collective-permute-start | bytes 786440 | tf_op jit(solution)/shard_map/ppermute | solution.py:11
  57.2 20.5 %collective-permute-done.1 = f32[512,512]{1,0:T(8,128)} collective-permute-done((f32[512,512]{1,0:T(8,128)S(1)}, f32[512,512]{1,0:T(8,128)}, u32[]{:S(2)}, u32[]{:S(2)}) %collective-permute-start.1) | collective-permute-done | bytes 1048608 | tf_op jit(solution)/shard_map/ppermute | solution.py:22
  77.7 2.0 %collective-permute-done = f32[512,512]{1,0:T(8,128)} collective-permute-done((f32[512,512]{1,0:T(8,128)S(1)}, f32[512,512]{1,0:T(8,128)}, u32[]{:S(2)}, u32[]{:S(2)}) %collective-permute-start) | collective-permute-done | bytes 1048608 | tf_op jit(solution)/shard_map/ppermute | solution.py:21
  79.7 3.5 %pad_maximum_fusion = f32[1536,512]{1,0:T(8,128)} fusion(f32[512,512]{1,0:T(8,128)} %collective-permute-done.1, f32[512,512]{1,0:T(8,128)S(1)} %gather_fusion, f32[512,512]{1,0:T(8,128)} %collective-permute-done), kind=kLoop, calls=%fused_computation.3 | loop fusion | flops 1572864 | bytes 6291456 | tf_op jit(solution)/shard_map/concatenate | solution.py:23
  83.3 5.1 %gather_fusion.1 = f32[20,128,512]{2,1,0:T(8,128)} fusion(f32[12,128,512]{2,1,0:T(8,128)} %bitcast.129, s32[1024]{0:T(1024)S(1)} %pad_clamp_fusion), kind=kCustom, calls=%fused_computation.1 | custom fusion | bytes 10485840 | tf_op jit(solution)/shard_map/gather | solution.py:31
  88.3 5.2 %fusion.69 = f32[4,512,128,1]{1,2,3,0:T(8,128)S(1)} fusion(f32[4,5,128,512]{3,2,1,0:T(8,128)} %bitcast.130, f32[4,5,128,128]{3,2,1,0:T(8,128)S(1)} %copy-done), kind=kOutput, calls=%fused_computation.101 | convolution fusion | flops 2013265920 | bytes 7602176 | tf_op jit(solution)/shard_map/jbrc,jbcn->jrn/dot_general | solution.py:32
  93.9 1.4 %fusion.27 = f32[128,512]{1,0:T(8,128)S(1)} fusion(f32[128,512]{0,1:T(8,128)} %collective-permute-done.6, f32[128,128]{0,1:T(8,128)} %copy.19, pred[]{:T(512)S(6)} %eq.35, f32[5,128,128]{2,1,0:T(8,128)} %param.15), kind=kOutput, calls=%fused_computation.42 | convolution fusion | flops 100679680 | bytes 655361 | tf_op jit(solution)/shard_map/dot_general | solution.py:42
  95.4 1.3 %fusion.29 = f32[128,512]{1,0:T(8,128)S(1)} fusion(f32[128,512]{1,0:T(8,128)S(1)} %fusion.27, f32[4,2,128,128]{3,2,1,0:T(8,128)} %param.14, pred[]{:T(512)S(6)} %eq.34), kind=kOutput, calls=%fused_computation.45 | convolution fusion | flops 100679680 | bytes 655361 | tf_op jit(solution)/shard_map/dot_general | solution.py:86
  96.7 1.4 %convolution_add_fusion.1 = f32[128,512]{1,0:T(8,128)S(1)} fusion(f32[128,512]{1,0:T(8,128)S(1)} %fusion.29, f32[128,512]{0,1:T(8,128)} %copy-done.6, f32[128,128]{0,1:T(8,128)} %copy.18, pred[]{:T(512)S(6)} %eq.33, f32[5,128,128]{2,1,0:T(8,128)} %param.15), kind=kOutput, calls=%fused_computation.8 | convolution fusion | flops 100745216 | bytes 917505 | tf_op jit(solution)/shard_map/dot_general | solution.py:42
  98.1 1.2 %fusion.33 = f32[128,512]{1,0:T(8,128)S(1)} fusion(f32[128,512]{1,0:T(8,128)S(1)} %convolution_add_fusion.1, f32[4,2,128,128]{3,2,1,0:T(8,128)} %param.14, pred[]{:T(512)S(6)} %eq.32), kind=kOutput, calls=%fused_computation.51 | convolution fusion | flops 100679680 | bytes 655361 | tf_op jit(solution)/shard_map/dot_general | solution.py:86
  99.4 1.4 %convolution_add_fusion.3 = f32[128,512]{1,0:T(8,128)S(1)} fusion(f32[128,512]{1,0:T(8,128)S(1)} %fusion.33, f32[128,512]{0,1:T(8,128)} %copy-done.5, f32[128,128]{0,1:T(8,128)} %copy.17, pred[]{:T(512)S(6)} %eq.31, f32[5,128,128]{2,1,0:T(8,128)} %param.15), kind=kOutput, calls=%fused_computation.11 | convolution fusion | flops 100745216 | bytes 917505 | tf_op jit(solution)/shard_map/dot_general | solution.py:42
  103.3 1.2 %fusion.41 = f32[128,512]{1,0:T(8,128)S(1)} fusion(f32[128,512]{1,0:T(8,128)S(1)} %convolution_add_fusion.5, f32[4,2,128,128]{3,2,1,0:T(8,128)} %param.14, pred[]{:T(512)S(6)} %eq.28), kind=kOutput, calls=%fused_computation.63 | convolution fusion | flops 100679680 | bytes 655361 | tf_op jit(solution)/shard_map/dot_general | solution.py:86
  107.1 3.2 %scatter_custom_fusion = f32[512,512]{1,0:T(8,128)} fusion(s32[512]{0:T(512)S(1)} %bitcast.133, f32[512,512]{1,0:T(8,128)S(1)} %copy.21, f32[]{:T(128)} %constant.11.clone.1), kind=kCustom, calls=%fused_computation.19 | custom fusion | bytes 1048580 | tf_op jit(solution)/shard_map/scatter | solution.py:91
  (39 shorter events, 11.3 us)
Async XLA Ops:
  0.0 88.3 %copy-start = (f32[4,5,128,128]{3,2,1,0:T(8,128)S(1)}, f32[4,5,128,128]{3,2,1,0:T(8,128)}, u32[]{:S(2)}) copy-start(f32[4,5,128,128]{3,2,1,0:T(8,128)} %param.12) | copy-start | bytes 3932164
  0.8 3.3 %copy-start.8 = (f32[512,128]{1,0:T(8,128)S(1)}, f32[512,128]{1,0:T(8,128)}, u32[]{:S(2)}) copy-start(f32[512,128]{1,0:T(8,128)} %param.9) | copy-start | bytes 786436
  4.1 33.1 %copy-start.9 = (s32[4,5]{1,0:T(4,128)S(1)}, s32[4,5]{1,0:T(4,128)}, u32[]{:S(2)}) copy-start(s32[4,5]{1,0:T(4,128)} %param.13) | copy-start | bytes 244
  5.9 9.3 %collective-permute-start.2 = (f32[128,512]{0,1:T(8,128)S(1)}, f32[128,512]{0,1:T(8,128)S(1)}, u32[]{:S(2)}, u32[]{:S(2)}) collective-permute-start(f32[128,512]{0,1:T(8,128)S(1)} %convolution_bitcast_fusion.1), channel_id=1, source_target_pairs={{0,1},{1,0},{2,3},{3,2},{4,5},{5,4},{6,7},{7,6},{8,9},{9,8},{10,11... | collective-permute-start | bytes 786440 | tf_op jit(solution)/shard_map/ppermute | solution.py:11
  15.3 31.4 %copy-start.1 = (f32[128,512]{0,1:T(8,128)}, f32[128,512]{0,1:T(8,128)S(1)}, u32[]{:S(2)}) copy-start(f32[128,512]{0,1:T(8,128)S(1)} %collective-permute-done.2) | copy-start | bytes 786436
  17.8 7.5 %collective-permute-start.3 = (f32[128,512]{0,1:T(8,128)S(1)}, f32[128,512]{0,1:T(8,128)S(1)}, u32[]{:S(2)}, u32[]{:S(2)}) collective-permute-start(f32[128,512]{0,1:T(8,128)S(1)} %fusion.4), channel_id=1, source_target_pairs={{0,2},{1,3},{2,0},{3,1},{4,6},{5,7},{6,4},{7,5},{8,10},{9,11},{10,... | collective-permute-start | bytes 786440 | tf_op jit(solution)/shard_map/ppermute | solution.py:11
  25.3 30.5 %copy-start.3 = (f32[128,512]{0,1:T(8,128)}, f32[128,512]{0,1:T(8,128)S(1)}, u32[]{:S(2)}) copy-start(f32[128,512]{0,1:T(8,128)S(1)} %collective-permute-done.3) | copy-start | bytes 786436
  27.8 14.0 %collective-permute-start.4 = (f32[128,512]{0,1:T(8,128)S(1)}, f32[128,512]{0,1:T(8,128)S(1)}, u32[]{:S(2)}, u32[]{:S(2)}) collective-permute-start(f32[128,512]{0,1:T(8,128)S(1)} %fusion.3), channel_id=1, source_target_pairs={{0,4},{1,5},{2,6},{3,7},{4,0},{5,1},{6,2},{7,3},{8,12},{9,13},{10,... | collective-permute-start | bytes 786440 | tf_op jit(solution)/shard_map/ppermute | solution.py:11
  30.4 47.4 %collective-permute-start.1 = (f32[512,512]{1,0:T(8,128)S(1)}, f32[512,512]{1,0:T(8,128)}, u32[]{:S(2)}, u32[]{:S(2)}) collective-permute-start(f32[512,512]{1,0:T(8,128)S(1)} %gather_fusion), channel_id=1, source_target_pairs={{1,0},{2,1},{3,2},{4,3},{5,4},{6,5},{7,6},{8,7},{9,8},{10,9},{11,1... | collective-permute-start | bytes 3145736 | tf_op jit(solution)/shard_map/ppermute | solution.py:22
  31.7 48.1 %collective-permute-start = (f32[512,512]{1,0:T(8,128)S(1)}, f32[512,512]{1,0:T(8,128)}, u32[]{:S(2)}, u32[]{:S(2)}) collective-permute-start(f32[512,512]{1,0:T(8,128)S(1)} %gather_fusion), channel_id=1, source_target_pairs={{0,1},{1,2},{2,3},{3,4},{4,5},{5,6},{6,7},{7,8},{8,9},{9,10},{10,1... | collective-permute-start | bytes 3145736 | tf_op jit(solution)/shard_map/ppermute | solution.py:21
  41.8 46.5 %copy-start.5 = (f32[128,512]{0,1:T(8,128)}, f32[128,512]{0,1:T(8,128)S(1)}, u32[]{:S(2)}) copy-start(f32[128,512]{0,1:T(8,128)S(1)} %collective-permute-done.4) | copy-start | bytes 786436
  45.0 7.4 %collective-permute-start.5 = (f32[128,512]{0,1:T(8,128)}, f32[128,512]{0,1:T(8,128)S(1)}, u32[]{:S(2)}, u32[]{:S(2)}) collective-permute-start(f32[128,512]{0,1:T(8,128)} %fusion.2), channel_id=1, source_target_pairs={{0,8},{8,0},{16,24},{24,16},{1,9},{9,1},{17,25},{25,17},{2,10},{10... | collective-permute-start | bytes 786440 | tf_op jit(solution)/shard_map/ppermute | solution.py:11
  52.4 35.9 %copy-start.6 = (f32[128,512]{0,1:T(8,128)}, f32[128,512]{0,1:T(8,128)S(1)}, u32[]{:S(2)}) copy-start(f32[128,512]{0,1:T(8,128)S(1)} %collective-permute-done.5) | copy-start | bytes 786436
  55.8 38.2 %collective-permute-start.6 = (f32[128,512]{0,1:T(8,128)}, f32[128,512]{0,1:T(8,128)}, u32[]{:S(2)}, u32[]{:S(2)}) collective-permute-start(f32[128,512]{0,1:T(8,128)} %fusion.1), channel_id=1, source_target_pairs={{0,16},{8,24},{16,0},{24,8},{1,17},{9,25},{17,1},{25,9},{2,18},{10... | collective-permute-start | bytes 786440 | tf_op jit(solution)/shard_map/ppermute | solution.py:11
  93.9 8.1 %copy-start.4 = (f32[128,512]{0,1:T(8,128)S(1)}, f32[128,512]{0,1:T(8,128)}, u32[]{:S(2)}) copy-start(f32[128,512]{0,1:T(8,128)} %copy-done.3) | copy-start | bytes 786436
  93.9 10.6 %copy-start.2 = (f32[128,512]{0,1:T(8,128)S(1)}, f32[128,512]{0,1:T(8,128)}, u32[]{:S(2)}) copy-start(f32[128,512]{0,1:T(8,128)} %copy-done.1) | copy-start | bytes 786436
  95.4 10.4 %copy-start.7 = (f32[512,128]{1,0:T(8,128)S(1)}, f32[512,128]{1,0:T(8,128)}, u32[]{:S(2)}) copy-start(f32[512,128]{1,0:T(8,128)} %param.10) | copy-start | bytes 786436
where the time goes:
time: 112 us; the launch traced here: 110 us
  waiting for transfers between devices  38.9 us (35%)
  matrix products  31.2 us (28%)
  local copies, waits for them, and re-layouts  19.8 us (18%)
  starting transfers between devices  15.8 us (14%)
  other arithmetic  4.32 us (4%)
    ppermute x1, waiting for transfers between devices, extended(): after = lax.ppermute(initial, axis, down)  20.5 us
    ppermute x5, waiting for transfers between devices, from_partner(): lax.ppermute(x, axis, [(i, i ^ 1 << bit) for i in range(lax.axis_size(axi...  16.4 us
    ppermute x5, starting transfers between devices, from_partner(): lax.ppermute(x, axis, [(i, i ^ 1 << bit) for i in range(lax.axis_size(axi...  9.02 us
    squeeze x6, local copies, waits for them, and re-layouts, sibling_step(): chosen = jnp.where(on_left, coupling[level], coupling[level].T)  7.4 us
    dot_general x5, matrix products, sibling_step(): coupled = jnp.dot(chosen, sibling, precision=exact)  6.71 us
    dot_general x4, matrix products, sibling_step(): jnp.dot(transfer[level, 0].T, left_node, precision=exact)  6.36 us
    ppermute x1, starting transfers between devices, extended(): before = lax.ppermute(last, axis, up)  5.54 us
    dot_general x1, matrix products, near_field(): jnp.einsum('jbrc,jbcn->jrn', blocks_here, taken, precision=lax.Precision....  5.23 us
  transfers between devices with their start and end apart: 7, of which 5 were waited for; matrix products, arithmetic and copies ran while one was open for 25% of the time, Pallas kernels for 0%

commit v1 on v0

v1 whole, which is shorter than its diff:
```python
import functools

import jax
import jax.numpy as jnp
from jax import lax
from jax.experimental import pallas as pl
from jax.experimental.pallas import tpu as pltpu
from jax.sharding import PartitionSpec as P

BLK = 128
REACH = 4
AXES = ("gx", "gy")
CHUNKS = (2, 2)
F32 = jnp.float32
BF16 = jnp.bfloat16


def split(x):
    high = x.astype(BF16)
    return high, (x - high.astype(F32)).astype(BF16)


def left_parts(x, axis):
    high, low = split(x)
    return jnp.concatenate([high, low, high], axis=axis)


def right_parts(x, axis):
    high, low = split(x)
    return jnp.concatenate([high, high, low], axis=axis)


def mm(a, b):
    return lax.dot_general(a, b, (((1,), (0,)), ((), ())), preferred_element_type=F32)


def mm_t(a, b):
    return lax.dot_general(a, b, (((1,), (1,)), ((), ())), preferred_element_type=F32)


def pick_rows(perm_row):
    length = perm_row.shape[1]
    column = jnp.transpose(jnp.broadcast_to(perm_row, (BLK, length)))
    parts = []
    for c in range(length // BLK):
        lanes = lax.broadcasted_iota(jnp.int32, (length, BLK), 1) + c * BLK
        parts.append(jnp.where(column == lanes, 1.0, 0.0).astype(BF16))
    return jnp.concatenate(parts, axis=1)


def place_rows(perm_row):
    length = perm_row.shape[1]
    rows = lax.broadcasted_iota(jnp.int32, (length, length), 0)
    return jnp.where(rows == perm_row, 1.0, 0.0).astype(BF16)


def first_kernel(perm_ref, x_ref, basis_ref, skel_ref, *chunk_refs):
    width = x_ref.shape[1]
    high, low = split(x_ref[...])
    both = mm(pick_rows(perm_ref[...]), jnp.concatenate([high, low], axis=1))
    tree = both[:, :width] + both[:, width:]
    start = 0
    for ref in chunk_refs:
        ref[...] = tree[start : start + ref.shape[0]]
        start += ref.shape[0]
    basis = left_parts(jnp.transpose(basis_ref[...]), 1)
    skel = mm(basis, right_parts(tree, 0))
    skel_ref[...] = jnp.transpose(skel)


def weights_kernel(transfer_ref, coupling_ref, left_ref, right_ref, down_ref):
    levels = coupling_ref.shape[0]
    for m in range(levels):
        couple = coupling_ref[m]
        t = min(m, levels - 2)
        left = jnp.concatenate([transfer_ref[t, 0], couple], axis=1)
        right = jnp.concatenate([transfer_ref[t, 1], jnp.transpose(couple)], axis=1)
        left_ref[m] = right_parts(left, 0)
        right_ref[m] = right_parts(right, 0)
        if m < levels - 1:
            down = jnp.concatenate(
                [jnp.transpose(transfer_ref[m, 0]), jnp.transpose(transfer_ref[m, 1])], axis=1
            )
            down_ref[m] = right_parts(down, 0)


def tree_kernel(width, s_ref, left_ref, right_ref, down_ref, e_ref):
    levels = left_ref.shape[0]
    rank = s_ref.shape[1]
    nodes = s_ref[...]
    couples = []
    for m in range(levels):
        pairs = nodes.reshape(-1, 2, width, rank)
        lefts = left_parts(pairs[:, 0].reshape(-1, rank), 1)
        rights = left_parts(pairs[:, 1].reshape(-1, rank), 1)
        from_left = mm(lefts, left_ref[m])
        from_right = mm(rights, right_ref[m])
        nodes = from_left[:, :rank] + from_right[:, :rank]
        couples.append((from_right[:, rank:], from_left[:, rank:]))

    def joined(a, b):
        a = a.reshape(-1, 1, width, rank)
        b = b.reshape(-1, 1, width, rank)
        return jnp.concatenate([a, b], axis=1).reshape(-1, rank)

    expand = joined(*couples[levels - 1])
    for m in range(levels - 2, -1, -1):
        down = mm(left_parts(expand, 1), down_ref[m])
        expand = joined(couples[m][0] + down[:, :rank], couples[m][1] + down[:, rank:])
    e_ref[...] = expand


def tree_plain(s, transfer, coupling, width):
    exact = lax.Precision.HIGHEST
    levels, rank = coupling.shape[:2]
    nodes = s
    couples = []
    for m in range(levels):
        pairs = nodes.reshape(-1, 2, width, rank)
        left, right = pairs[:, 0], pairs[:, 1]
        to_left = jnp.einsum("pnk,rk->pnr", right, coupling[m], precision=exact)
        to_right = jnp.einsum("pnk,kr->pnr", left, coupling[m], precision=exact)
        couples.append(jnp.stack([to_left, to_right], 1))
        if m < levels - 1:
            nodes = jnp.einsum("pnk,kr->pnr", left, transfer[m, 0], precision=exact)
            nodes = nodes + jnp.einsum("pnk,kr->pnr", right, transfer[m, 1], precision=exact)
    expand = couples[levels - 1]
    for m in range(levels - 2, -1, -1):
        parent = expand.reshape(-1, width, rank)
        down = jnp.einsum("pnk,srk->psnr", parent, transfer[m], precision=exact)
        expand = couples[m] + down
    return expand.reshape(-1, rank)


def last_kernel(n_chunks, offsets_ref, perm_ref, blocks_ref, basis_ref, expand_ref, *rest):
    own_refs = rest[:n_chunks]
    sib_refs = rest[n_chunks : 2 * n_chunks]
    fwd_refs = rest[2 * n_chunks : 3 * n_chunks]
    out_ref, high_ref, low_ref, acc_ref = rest[3 * n_chunks :]
    n_rows, n_band = offsets_ref.shape
    slot = 0
    for refs in (own_refs, sib_refs, fwd_refs):
        for ref in refs:
            for c in range(ref.shape[0] // BLK):
                high, low = split(ref[c * BLK : (c + 1) * BLK, :])
                high_ref[slot] = high
                low_ref[slot] = low
                slot += 1
    odd = lax.rem(lax.axis_index("gy"), 2)
    left_base = jnp.where(odd == 1, n_rows, 2 * n_rows)
    right_base = jnp.where(odd == 1, 2 * n_rows, n_rows)
    expand = right_parts(expand_ref[...], 1)
    for i in range(n_rows):
        rows = slice(i * BLK, (i + 1) * BLK)
        total = mm_t(left_parts(basis_ref[rows, :], 1), expand)
        for j in range(n_band):
            t = offsets_ref[i, j] + i
            at = jnp.where(
                t < 0, left_base + t + n_rows, jnp.where(t < n_rows, t, right_base + t - n_rows)
            )
            high = high_ref[at]
            low = low_ref[at]
            total += mm(
                left_parts(blocks_ref[i, j], 1), jnp.concatenate([high, high, low], axis=0)
            )
        acc_ref[rows, :] = total
    high, low = split(acc_ref[...])
    width = out_ref.shape[1]
    both = mm(place_rows(perm_ref[...]), jnp.concatenate([high, low], axis=1))
    out_ref[...] = both[:, :width] + both[:, width:]


def vmem(n):
    return [pl.BlockSpec(memory_space=pltpu.VMEM)] * n


def per_device(
    columns, col_basis, row_basis, order_perm, near_blocks, band_offsets, transfer, coupling
):
    across, along = lax.axis_size("gx"), lax.axis_size("gy")
    devices = across * along
    leaf, width = columns.shape
    rank = col_basis.shape[1]
    levels = coupling.shape[0]
    n_rows = leaf // BLK
    share = width // devices
    sibling = [(d, d ^ 1) for d in range(devices)]
    forward = []
    for d in range(devices):
        held = d ^ 1
        to = held + 1 if held % 2 else held - 1
        if 0 <= to < devices:
            forward.append((d, to))

    chunk_shapes = [jax.ShapeDtypeStruct((c * BLK, width), F32) for c in CHUNKS]
    first = pl.pallas_call(
        first_kernel,
        out_shape=[jax.ShapeDtypeStruct((width, rank), F32)] + chunk_shapes,
        in_specs=vmem(3),
        out_specs=vmem(1 + len(CHUNKS)),
        name="first",
    )(order_perm, columns, col_basis)
    skel, own = first[0], first[1:]

    sib = [lax.ppermute(c, AXES, sibling) for c in own]
    fwd = [lax.ppermute(c, AXES, forward) for c in sib]

    gathered = lax.all_to_all(skel.reshape(devices, share, rank), AXES, 0, 0)
    gathered = gathered.reshape(width, rank)
    if share % 8 == 0:
        weights = pl.pallas_call(
            weights_kernel,
            out_shape=[
                jax.ShapeDtypeStruct((levels, 3 * rank, 2 * rank), BF16),
                jax.ShapeDtypeStruct((levels, 3 * rank, 2 * rank), BF16),
                jax.ShapeDtypeStruct((levels - 1, 3 * rank, 2 * rank), BF16),
            ],
            in_specs=vmem(2),
            out_specs=vmem(3),
            name="weights",
        )(transfer, coupling)
        expand = pl.pallas_call(
            functools.partial(tree_kernel, share),
            out_shape=jax.ShapeDtypeStruct((width, rank), F32),
            in_specs=vmem(4),
            out_specs=vmem(1)[0],
            name="tree",
        )(gathered, *weights)
    else:
        expand = tree_plain(gathered, transfer, coupling, share)
    expand = lax.all_to_all(expand.reshape(devices, share, rank), AXES, 0, 0)
    expand = expand.reshape(width, rank)

    return pl.pallas_call(
        functools.partial(last_kernel, len(CHUNKS)),
        out_shape=jax.ShapeDtypeStruct((leaf, width), F32),
        in_specs=[pl.BlockSpec(memory_space=pltpu.SMEM)] + vmem(4 + 3 * len(CHUNKS)),
        out_specs=vmem(1)[0],
        scratch_shapes=[
            pltpu.VMEM((3 * leaf // BLK, BLK, width), BF16),
            pltpu.VMEM((3 * leaf // BLK, BLK, width), BF16),
            pltpu.VMEM((leaf, width), F32),
        ],
        name="last",
    )(band_offsets, order_perm, near_blocks, row_basis, expand, *own, *sib, *fwd)


def solution(mesh):
    placed = (
        P(("gx", "gy"), None),
        P(("gx", "gy"), None),
        P(("gx", "gy"), None),
        P(("gx", "gy"), None),
        P(("gx", "gy"), None, None, None),
        P(("gx", "gy"), None),
        P(),
        P(),
    )
    return jax.shard_map(
        per_device, mesh=mesh, in_specs=placed, out_specs=P(("gx", "gy"), None), check_vma=False
    )
```

time: 112 us -> 66.7 us (0.60); the launches traced: 110 us -> 66.3 us
  matrix products: 31.2 us -> 0 us
  waiting for transfers between devices: 38.9 us -> 15.1 us
  local copies, waits for them, and re-layouts: 19.8 us -> 1.66 us
  Pallas kernels: 0 us -> 16.8 us
  blocking collectives: 0 us -> 15.3 us
  other arithmetic: 4.32 us -> 0 us
  starting transfers between devices: 15.8 us -> 17.4 us
    dot_general x20 -> x0, matrix products: 31.2 us -> none  [the longest x5 6.71 us: sibling_step(): coupled = jnp.dot(chosen, sibling, precision=exact)]
    ppermute x7 -> x4, waiting for transfers between devices: 38.9 us -> 15.1 us  [the longest x2 15.1 us: per_device(): sib = [lax.ppermute(c, AXES, sibling) for c in own]]
    pallas_call x0 -> x4, Pallas kernels: none -> 16.8 us  [the longest x1 6.57 us: per_device(): pl.pallas_call(functools.partial(last_kernel, len(CHUNKS)), out_shape=jax...]
    all_to_all x0 -> x1, blocking collectives: none -> 15.3 us  [per_device(): expand = lax.all_to_all(expand.reshape(devices, share, rank), AXES, 0, 0)]
    gather x2 -> x0, local copies, waits for them, and re-layouts: 8.37 us -> none  [the longest x1 5.07 us: near_field(): taken = column_blocks[block_index]]
    squeeze x6 -> x0, local copies, waits for them, and re-layouts: 7.4 us -> none  [sibling_step(): chosen = jnp.where(on_left, coupling[level], coupling[level].T)]
    all_to_all x0 -> x1, starting transfers between devices: none -> 6.37 us  [per_device(): gathered = lax.all_to_all(skel.reshape(devices, share, rank), AXES, 0, 0)]
    ppermute x7 -> x4, starting transfers between devices: 15.8 us -> 11 us  [the longest x2 8.04 us: per_device(): fwd = [lax.ppermute(c, AXES, forward) for c in sib]]
  transfers between devices with their start and end apart: 7 -> 5, of which waited for: 5 -> 2; matrix products, arithmetic and copies ran while one was open for 25% -> 0% of each run, Pallas kernels for 0% -> 11%
where the time goes in v1:
time: 66.7 us; the launch traced here: 66.3 us
  starting transfers between devices  17.4 us (26%)
  Pallas kernels  16.8 us (25%)
  blocking collectives  15.3 us (23%)
  waiting for transfers between devices  15.1 us (23%)
  local copies, waits for them, and re-layouts  1.66 us (2%)
    all_to_all x1, blocking collectives, per_device(): expand = lax.all_to_all(expand.reshape(devices, share, rank), AXES, 0, 0)  15.3 us
    ppermute x2, waiting for transfers between devices, per_device(): sib = [lax.ppermute(c, AXES, sibling) for c in own]  15.1 us
    ppermute x2, starting transfers between devices, per_device(): fwd = [lax.ppermute(c, AXES, forward) for c in sib]  8.04 us
    pallas_call x1, Pallas kernels, per_device(): pl.pallas_call(functools.partial(last_kernel, len(CHUNKS)), out_shape=jax...  6.57 us
    all_to_all x1, starting transfers between devices, per_device(): gathered = lax.all_to_all(skel.reshape(devices, share, rank), AXES, 0, 0)  6.37 us
    pallas_call x1, Pallas kernels, per_device(): pl.pallas_call(functools.partial(tree_kernel, share), out_shape=jax.Shape...  4.13 us
    pallas_call x1, Pallas kernels, per_device(): pl.pallas_call(first_kernel, out_shape=[jax.ShapeDtypeStruct((width, rank...  3.25 us
    ppermute x2, starting transfers between devices, per_device(): sib = [lax.ppermute(c, AXES, sibling) for c in own]  2.99 us
  transfers between devices with their start and end apart: 5, of which 2 were waited for; matrix products, arithmetic and copies ran while one was open for 0% of the time, Pallas kernels for 11%

profile of v1, /device:TPU:0, one launch (start us, length us, event | category | flops | bytes accessed | tf_op | source)
XLA Modules:
  0.0 66.3 jit_solution(13372327010038929264)
XLA Ops:
  0.0 3.3 %first.1 = (f32[512,128]{1,0:T(8,128)}, f32[256,512]{1,0:T(8,128)}, f32[256,512]{1,0:T(8,128)}) custom-call(s32[1,512]{1,0:T(1,128)} %perm_ref.3, f32[512,512]{1,0:T(8,128)} %x_ref.1, f32[512,128]{1,0:T(8,128)} %basis_ref.2), custom_call_target="tpu_custom_call" | custom-call | tf_op jit(solution)/shard_map/first/pallas_call | solution.py:196
  3.3 3.0 %collective-permute-start = (f32[256,512]{1,0:T(8,128)}, f32[256,512]{1,0:T(8,128)S(1)}, u32[]{:S(2)}, u32[]{:S(2)}) collective-permute-start(f32[256,512]{1,0:T(8,128)} %get-tuple-element.15.rest_0_), channel_id=1, source_target_pairs={{0,1},{1,0},{2,3},{3,2},{4,5},{5,4},{6,7},{7,6},{8,9},{9,8},{10,11... | collective-permute-start | bytes 1572872 | tf_op jit(solution)/shard_map/ppermute | solution.py:205
  6.2 0.0 collective-permute-start.1
  6.2 6.4 %all-to-all-start = ((f32[32,16,128]{2,1,0:T(8,128)}), f32[32,16,128]{2,1,0:T(8,128)S(1)}, u32[]{:S(2)}, u32[]{:S(2)}) async-start(f32[32,16,128]{2,1,0:T(8,128)} %bitcast.7), calls=%async_computation | async-start | bytes 524288 | tf_op jit(solution)/shard_map/all_to_all | solution.py:208
  12.6 8.4 %collective-permute-done.rest_2_ = f32[256,512]{1,0:T(8,128)S(1)} collective-permute-done((f32[256,512]{1,0:T(8,128)}, f32[256,512]{1,0:T(8,128)S(1)}, u32[]{:S(2)}, u32[]{:S(2)}) %collective-permute-start) | collective-permute-done | bytes 524320 | tf_op jit(solution)/shard_map/ppermute | solution.py:205
  21.1 0.0 copy-start.1
  21.1 4.3 %collective-permute-start.2 = (f32[256,512]{1,0:T(8,128)S(1)}, f32[256,512]{1,0:T(8,128)S(1)}, u32[]{:S(2)}, u32[]{:S(2)}) collective-permute-start(f32[256,512]{1,0:T(8,128)S(1)} %collective-permute-done.rest_2_), channel_id=1, source_target_pairs={{0,2},{2,4},{3,1},{4,6},{5,3},{6,8},{7,5},{8,10},{9,7},{10,12},{11... | collective-permute-start | bytes 1572872 | tf_op jit(solution)/shard_map/ppermute | solution.py:206
  25.4 6.7 %collective-permute-done.1.rest_3_ = f32[256,512]{1,0:T(8,128)S(1)} collective-permute-done((f32[256,512]{1,0:T(8,128)}, f32[256,512]{1,0:T(8,128)S(1)}, u32[]{:S(2)}, u32[]{:S(2)}) %collective-permute-start.1) | collective-permute-done | bytes 524320 | tf_op jit(solution)/shard_map/ppermute | solution.py:205
  32.1 0.0 copy-start.2
  32.1 3.7 %collective-permute-start.3 = (f32[256,512]{1,0:T(8,128)S(1)}, f32[256,512]{1,0:T(8,128)S(1)}, u32[]{:S(2)}, u32[]{:S(2)}) collective-permute-start(f32[256,512]{1,0:T(8,128)S(1)} %collective-permute-done.1.rest_3_), channel_id=1, source_target_pairs={{0,2},{2,4},{3,1},{4,6},{5,3},{6,8},{7,5},{8,10},{9,7},{10,12},{11... | collective-permute-start | bytes 1572872 | tf_op jit(solution)/shard_map/ppermute | solution.py:206
  35.8 2.9 %weights.1 = (bf16[5,384,256]{2,1,0:T(8,128)(2,1)}, bf16[5,384,256]{2,1,0:T(8,128)(2,1)}, bf16[4,384,256]{2,1,0:T(8,128)(2,1)}) custom-call(f32[4,2,128,128]{3,2,1,0:T(8,128)} %transfer_ref.1, f32[5,128,128]{2,1,0:T(8,128)} %coupling_ref.1), custom_call_target="tpu_custom_call" | custom-call | tf_op jit(solution)/shard_map/weights/pallas_call | solution.py:211
  38.7 0.0 all-to-all-done
  38.7 0.0 copy-start
  38.7 0.7 %copy-done = f32[32,16,128]{2,1,0:T(8,128)} copy-done((f32[32,16,128]{2,1,0:T(8,128)}, f32[32,16,128]{2,1,0:T(8,128)S(1)}, u32[]{:S(2)}) %copy-start) | copy-done | bytes 262168
  39.4 4.1 %tree.1 = f32[512,128]{1,0:T(8,128)} custom-call(f32[512,128]{1,0:T(8,128)} %bitcast.4, bf16[5,384,256]{2,1,0:T(8,128)(2,1)} %get-tuple-element.12.left_ref, bf16[5,384,256]{2,1,0:T(8,128)(2,1)} %get-tuple-element.13.right_ref, bf16[4,384,256]{2,1,0:T(8,128)(2,1)} %get-tuple-element.14.down_ref), custom_call_target="tpu_custom_call" | custom-call | tf_op jit(solution)/shard_map/tree/pallas_call | solution.py:222
  43.5 0.0 copy-done.1
  43.5 15.3 %all_to_all.10 = f32[32,16,128]{2,1,0:T(8,128)} all-to-all(f32[32,16,128]{2,1,0:T(8,128)} %bitcast.6), channel_id=1, replica_groups=mesh['gx'=4,'gy'=8] {'gx','gy'}, dimensions={0} | all-to-all | bytes 524288 | tf_op jit(solution)/shard_map/all_to_all | solution.py:231
  58.8 0.0 collective-permute-done.2.rest_4_
  58.8 0.0 copy-start.3
  58.8 0.0 collective-permute-done.3.rest_5_
  58.8 0.0 copy-start.4
  58.8 0.0 copy-done.2
  58.8 0.8 %copy-done.3 = f32[256,512]{1,0:T(8,128)} copy-done((f32[256,512]{1,0:T(8,128)}, f32[256,512]{1,0:T(8,128)S(1)}, u32[]{:S(2)}) %copy-start.3) | copy-done | bytes 524312
  59.6 0.2 copy-done.4
  59.8 6.6 %last.1 = f32[512,512]{1,0:T(8,128)} custom-call(s32[4,5]{1,0:T(4,128)} %offsets_ref.1, s32[1,512]{1,0:T(1,128)} %perm_ref.3, f32[4,5,128,128]{3,2,1,0:T(8,128)} %blocks_ref.1, f32[512,128]{1,0:T(8,128)} %basis_ref.3, f32[512,128]{1,0:T(8,128)} %bitcast.5, f32[256,512]{1,0:T(8,128)} %get-tuple-element.15.rest_0_, f32[256,512]{1,0:T(8,128)} %get-tuple-element.16.rest_1_, ...), custom_call_target="tpu_custom_call" | custom-call | tf_op jit(solution)/shard_map/last/pallas_call | solution.py:234
Async XLA Ops:
  3.3 17.8 %collective-permute-start = (f32[256,512]{1,0:T(8,128)}, f32[256,512]{1,0:T(8,128)S(1)}, u32[]{:S(2)}, u32[]{:S(2)}) collective-permute-start(f32[256,512]{1,0:T(8,128)} %get-tuple-element.15.rest_0_), channel_id=1, source_target_pairs={{0,1},{1,0},{2,3},{3,2},{4,5},{5,4},{6,7},{7,6},{8,9},{9,8},{10,11... | collective-permute-start | bytes 1572872 | tf_op jit(solution)/shard_map/ppermute | solution.py:205
  6.2 25.8 %collective-permute-start.1 = (f32[256,512]{1,0:T(8,128)}, f32[256,512]{1,0:T(8,128)S(1)}, u32[]{:S(2)}, u32[]{:S(2)}) collective-permute-start(f32[256,512]{1,0:T(8,128)} %get-tuple-element.16.rest_1_), channel_id=1, source_target_pairs={{0,1},{1,0},{2,3},{3,2},{4,5},{5,4},{6,7},{7,6},{8,9},{9,8},{10,11... | collective-permute-start | bytes 1572872 | tf_op jit(solution)/shard_map/ppermute | solution.py:205
  6.2 32.4 %all-to-all-start = ((f32[32,16,128]{2,1,0:T(8,128)}), f32[32,16,128]{2,1,0:T(8,128)S(1)}, u32[]{:S(2)}, u32[]{:S(2)}) async-start(f32[32,16,128]{2,1,0:T(8,128)} %bitcast.7), calls=%async_computation | async-start | bytes 524288 | tf_op jit(solution)/shard_map/all_to_all | solution.py:208
  21.1 22.5 %copy-start.1 = (f32[256,512]{1,0:T(8,128)}, f32[256,512]{1,0:T(8,128)S(1)}, u32[]{:S(2)}) copy-start(f32[256,512]{1,0:T(8,128)S(1)} %collective-permute-done.rest_2_) | copy-start | bytes 1572868
  21.1 37.7 %collective-permute-start.2 = (f32[256,512]{1,0:T(8,128)S(1)}, f32[256,512]{1,0:T(8,128)S(1)}, u32[]{:S(2)}, u32[]{:S(2)}) collective-permute-start(f32[256,512]{1,0:T(8,128)S(1)} %collective-permute-done.rest_2_), channel_id=1, source_target_pairs={{0,2},{2,4},{3,1},{4,6},{5,3},{6,8},{7,5},{8,10},{9,7},{10,12},{11... | collective-permute-start | bytes 1572872 | tf_op jit(solution)/shard_map/ppermute | solution.py:206
  32.1 26.7 %copy-start.2 = (f32[256,512]{1,0:T(8,128)}, f32[256,512]{1,0:T(8,128)S(1)}, u32[]{:S(2)}) copy-start(f32[256,512]{1,0:T(8,128)S(1)} %collective-permute-done.1.rest_3_) | copy-start | bytes 1572868
  32.1 26.7 %collective-permute-start.3 = (f32[256,512]{1,0:T(8,128)S(1)}, f32[256,512]{1,0:T(8,128)S(1)}, u32[]{:S(2)}, u32[]{:S(2)}) collective-permute-start(f32[256,512]{1,0:T(8,128)S(1)} %collective-permute-done.1.rest_3_), channel_id=1, source_target_pairs={{0,2},{2,4},{3,1},{4,6},{5,3},{6,8},{7,5},{8,10},{9,7},{10,12},{11... | collective-permute-start | bytes 1572872 | tf_op jit(solution)/shard_map/ppermute | solution.py:206
  38.7 0.7 %copy-start = (f32[32,16,128]{2,1,0:T(8,128)}, f32[32,16,128]{2,1,0:T(8,128)S(1)}, u32[]{:S(2)}) copy-start(f32[32,16,128]{2,1,0:T(8,128)S(1)} %all-to-all-done) | copy-start | bytes 786436
  58.8 0.8 %copy-start.3 = (f32[256,512]{1,0:T(8,128)}, f32[256,512]{1,0:T(8,128)S(1)}, u32[]{:S(2)}) copy-start(f32[256,512]{1,0:T(8,128)S(1)} %collective-permute-done.2.rest_4_) | copy-start | bytes 1572868
  58.8 1.0 %copy-start.4 = (f32[256,512]{1,0:T(8,128)}, f32[256,512]{1,0:T(8,128)S(1)}, u32[]{:S(2)}) copy-start(f32[256,512]{1,0:T(8,128)S(1)} %collective-permute-done.3.rest_5_) | copy-start | bytes 1572868

commit v2 on v1

v2 whole, which is shorter than its diff:
```python
import functools

import jax
import jax.numpy as jnp
from jax import lax
from jax.experimental import pallas as pl
from jax.experimental.pallas import tpu as pltpu
from jax.sharding import PartitionSpec as P


BLK = 128
AXES = ("gx", "gy")
CHUNKS = ((1, False), (1, False), (2, False))
LATE = ('f2',)
OUT_COPIES = 8
PIECES = 4
TREE_MIB = 10
LAST_MIB = 14
F32 = jnp.float32
BF16 = jnp.bfloat16


def split(x):
    high = x.astype(BF16)
    return high, (x - high.astype(F32)).astype(BF16)


def left_parts(x, axis):
    high, low = split(x)
    return jnp.concatenate([high, low, high], axis=axis)


def right_parts(x, axis):
    high, low = split(x)
    return jnp.concatenate([high, high, low], axis=axis)


def mm(a, b):
    return lax.dot_general(a, b, (((1,), (0,)), ((), ())), preferred_element_type=F32)


def mm_t(a, b):
    return lax.dot_general(a, b, (((1,), (1,)), ((), ())), preferred_element_type=F32)


def pick_rows(perm_row):
    length = perm_row.shape[1]
    column = jnp.transpose(jnp.broadcast_to(perm_row, (BLK, length)))
    parts = []
    for c in range(length // BLK):
        lanes = lax.broadcasted_iota(jnp.int32, (length, BLK), 1) + c * BLK
        parts.append(jnp.where(column == lanes, 1.0, 0.0).astype(BF16))
    return jnp.concatenate(parts, axis=1)


def place_rows(perm_row):
    length = perm_row.shape[1]
    rows = lax.broadcasted_iota(jnp.int32, (length, length), 0)
    return jnp.where(rows == perm_row, 1.0, 0.0).astype(BF16)


def first_kernel(perm_ref, x_ref, basis_ref, skel_ref, *chunk_refs):
    high, low = split(x_ref[...])
    pick = pick_rows(perm_ref[...])
    tree = mm(jnp.concatenate([pick, pick], axis=1), jnp.concatenate([high, low], axis=0))
    start = 0
    for ref in chunk_refs:
        ref[...] = tree[start : start + ref.shape[0]]
        start += ref.shape[0]
    basis = left_parts(jnp.transpose(basis_ref[...]), 1)
    skel = mm(basis, right_parts(tree, 0))
    skel_ref[...] = jnp.transpose(skel)


class Stage:
    def __init__(self, refs, n_smem, n_in, n_out):
        self.smem, refs = refs[:n_smem], refs[n_smem:]
        self.source, refs = refs[:n_in], refs[n_in:]
        self.target, refs = refs[:n_out], refs[n_out:]
        self.inside, refs = refs[:n_in], refs[n_in:]
        self.outside, refs = refs[:n_out], refs[n_out:]
        *self.scratch, self.in_sems, self.out_sems = refs
        self.loads = [
            pltpu.make_async_copy(a, b, self.in_sems.at[n])
            for n, (a, b) in enumerate(zip(self.source, self.inside))
        ]
        for load in self.loads:
            load.start()
        self.pending = set(range(n_in))
        self.stores = []

    def get(self, n):
        if n in self.pending:
            self.pending.remove(n)
            self.loads[n].wait()
        return self.inside[n]

    def rows(self, numbers):
        return jnp.concatenate([self.get(n)[...] for n in numbers], axis=0)

    def put(self, n, value, start=None):
        at = () if start is None else (pl.ds(start, value.shape[0]),)
        held = self.outside[n].at[at] if at else self.outside[n]
        held[...] = value
        store = pltpu.make_async_copy(
            held,
            self.target[n].at[at] if at else self.target[n],
            self.out_sems.at[len(self.stores)],
        )
        store.start()
        self.stores.append(store)

    def finish(self):
        assert not self.pending
        for store in self.stores:
            store.wait()


def staged(body, inputs, out_shapes, smem=(), scratch=(), mib=None):
    sizes = (len(smem), len(inputs), len(out_shapes))

    def kernel(*refs):
        stage = Stage(refs, *sizes)
        body(stage)
        stage.finish()

    return pl.pallas_call(
        kernel,
        out_shape=[jax.ShapeDtypeStruct(shape, dtype) for shape, dtype in out_shapes],
        in_specs=[pl.BlockSpec(memory_space=pltpu.SMEM)] * len(smem) + hbm(len(inputs)),
        out_specs=hbm(len(out_shapes)),
        scratch_shapes=[pltpu.VMEM(a.shape, a.dtype) for a in inputs]
        + [pltpu.VMEM(shape, dtype) for shape, dtype in out_shapes]
        + list(scratch)
        + [pltpu.SemaphoreType.DMA((len(inputs),)), pltpu.SemaphoreType.DMA((OUT_COPIES,))],
        compiler_params=None if mib is None else limit(mib),
    )(*smem, *inputs)


def prep_kernel(near_slots, late_slots, stage):
    (offsets_ref,), (dense_ref,) = stage.smem, stage.scratch
    n_rows, n_band = offsets_ref.shape
    odd = lax.rem(lax.axis_index("gy"), 2)
    left_base = jnp.where(odd == 1, n_rows, 2 * n_rows)
    right_base = jnp.where(odd == 1, 2 * n_rows, n_rows)
    dense_ref[...] = jnp.zeros_like(dense_ref)
    blocks_ref = stage.get(0)
    for i in range(n_rows):
        rows = slice(i * BLK, (i + 1) * BLK)
        for j in range(n_band):
            t = offsets_ref[i, j] + i
            at = jnp.where(
                t < 0, left_base + t + n_rows, jnp.where(t < n_rows, t, right_base + t - n_rows)
            )
            dense_ref[at, rows, :] += blocks_ref[i, j]

    def joined(slots):
        return split(jnp.concatenate([dense_ref[at] for at in slots], axis=1))

    high, low = joined(near_slots)
    stage.put(1, jnp.stack([high, low]))
    high, low = joined(range(n_rows))
    stage.put(
        0,
        mm(
            jnp.concatenate([high, low, high], axis=1),
            right_parts(stage.rows(range(3, len(stage.inside))), 0),
        ),
    )
    place = place_rows(stage.get(1)[...])
    high, low = joined(late_slots)
    stage.put(2, jnp.stack([mm(place, high).astype(BF16), mm(place, low).astype(BF16)]))
    high, low = split(stage.get(2)[...])
    stage.put(3, jnp.stack([mm(place, high).astype(BF16), mm(place, low).astype(BF16)]))


def left_pair(ref, *at):
    high, low = ref[(*at, 0)], ref[(*at, 1)]
    return jnp.concatenate([high, low, high], axis=1)


def tree_kernel(width, stage):
    coupling_ref, transfer_ref = stage.get(1), stage.get(2)
    levels, rank = coupling_ref.shape[:2]
    down_c = [right_parts(coupling_ref[m], 1) for m in range(levels)]
    up_c = [right_parts(coupling_ref[m], 0) for m in range(levels)]
    up_t = [[right_parts(transfer_ref[m, h], 0) for h in range(2)] for m in range(levels - 1)]
    down_t = [[right_parts(transfer_ref[m, h], 1) for h in range(2)] for m in range(levels - 1)]
    nodes = stage.get(0)[...]
    couples = []
    for m in range(levels):
        pairs = nodes.reshape(-1, 2, width, rank)
        lefts = left_parts(pairs[:, 0].reshape(-1, rank), 1)
        rights = left_parts(pairs[:, 1].reshape(-1, rank), 1)
        couples.append((mm_t(rights, down_c[m]), mm(lefts, up_c[m])))
        if m < levels - 1:
            nodes = mm(lefts, up_t[m][0]) + mm(rights, up_t[m][1])

    def joined(a, b):
        a = a.reshape(-1, 1, width, rank)
        b = b.reshape(-1, 1, width, rank)
        return jnp.concatenate([a, b], axis=1).reshape(-1, rank)

    expand = joined(*couples[levels - 1])
    for m in range(levels - 2, -1, -1):
        parents = left_parts(expand, 1)
        left = mm_t(parents, down_t[m][0])
        right = mm_t(parents, down_t[m][1])
        expand = joined(couples[m][0] + left, couples[m][1] + right)
    stage.put(0, expand)


def tree_plain(s, transfer, coupling, width):
    exact = lax.Precision.HIGHEST
    levels, rank = coupling.shape[:2]
    nodes = s
    couples = []
    for m in range(levels):
        pairs = nodes.reshape(-1, 2, width, rank)
        left, right = pairs[:, 0], pairs[:, 1]
        to_left = jnp.einsum("pnk,rk->pnr", right, coupling[m], precision=exact)
        to_right = jnp.einsum("pnk,kr->pnr", left, coupling[m], precision=exact)
        couples.append(jnp.stack([to_left, to_right], 1))
        if m < levels - 1:
            nodes = jnp.einsum("pnk,kr->pnr", left, transfer[m, 0], precision=exact)
            nodes = nodes + jnp.einsum("pnk,kr->pnr", right, transfer[m, 1], precision=exact)
    expand = couples[levels - 1]
    for m in range(levels - 2, -1, -1):
        parent = expand.reshape(-1, width, rank)
        down = jnp.einsum("pnk,srk->psnr", parent, transfer[m], precision=exact)
        expand = couples[m] + down
    return expand.reshape(-1, rank)


def near_kernel(stage):
    total = mm(left_pair(stage.get(2)), right_parts(stage.rows(range(3, len(stage.inside))), 0))
    high, low = split(stage.get(1)[...] + total)
    both = jnp.concatenate([high, low], axis=0)
    place = place_rows(stage.get(0)[...])
    place = jnp.concatenate([place, place], axis=1)
    step = place.shape[0] // PIECES
    for start in range(0, place.shape[0], step):
        stage.put(0, mm(place[start : start + step], both), start)


def last_kernel(stage):
    expand = right_parts(stage.get(0)[...], 1)
    far = mm_t(left_pair(stage.get(1)), expand)
    left = left_pair(stage.get(2))
    rows = right_parts(stage.rows(range(4, len(stage.inside))), 0)
    sum_ref = stage.get(3)
    step = left.shape[0] // PIECES
    for start in range(0, left.shape[0], step):
        at = slice(start, start + step)
        stage.put(0, sum_ref[at, :] + far[at] + mm(left[at], rows), start)


def limit(mib):
    return pltpu.CompilerParams(vmem_limit_bytes=mib << 20)


def hbm(n):
    return [pl.BlockSpec(memory_space=pltpu.HBM)] * n


def vmem(n):
    return [pl.BlockSpec(memory_space=pltpu.VMEM)] * n


def body(
    columns, col_basis, row_basis, order_perm, near_blocks, band_offsets, transfer, coupling
):
    across, along = lax.axis_size("gx"), lax.axis_size("gy")
    devices = across * along
    leaf, width = columns.shape
    n_rows = leaf // BLK
    rank = col_basis.shape[1]
    share = width // devices
    sibling = [(d, d ^ 1) for d in range(devices)]
    diagonal = [(d, d + 1 if d % 2 else d - 1) for d in range(1, devices - 1)]
    forward = []
    for d in range(devices):
        to = d - 2 if d % 2 else d + 2
        if 0 <= to < devices:
            forward.append((d, to))

    rows = [c * leaf // sum(n for n, _ in CHUNKS) for c, _ in CHUNKS]
    chunk_shapes = [jax.ShapeDtypeStruct((n, width), F32) for n in rows]
    n_chunks = len(CHUNKS)
    first = pl.pallas_call(
        first_kernel,
        out_shape=[jax.ShapeDtypeStruct((width, rank), F32)] + chunk_shapes,
        in_specs=vmem(3),
        out_specs=vmem(1 + n_chunks),
        name="first",
    )(order_perm, columns, col_basis)
    skel, own = first[0], list(first[1:])

    pieces = {}
    start = 0
    for c, (blocks, direct) in enumerate(CHUNKS):
        sib = lax.ppermute(own[c], AXES, sibling)
        if direct:
            fwd = lax.ppermute(own[c], AXES, diagonal)
        else:
            fwd = lax.ppermute(sib, AXES, forward)
        blocks = rows[c] // BLK
        pieces[f"s{c}"] = (sib, range(n_rows + start, n_rows + start + blocks))
        pieces[f"f{c}"] = (fwd, range(2 * n_rows + start, 2 * n_rows + start + blocks))
        start += blocks
    early = [pieces[p] for p in pieces if p not in LATE]
    late = [pieces[p] for p in LATE]
    near_slots = [at for _, slots in early for at in slots]
    late_slots = [at for _, slots in late for at in slots]

    own_sum, near, left, far = staged(
        functools.partial(prep_kernel, near_slots, late_slots),
        [near_blocks, order_perm, row_basis] + own,
        [
            ((leaf, width), F32),
            ((2, leaf, len(near_slots) * BLK), BF16),
            ((2, leaf, len(late_slots) * BLK), BF16),
            ((2, leaf, rank), BF16),
        ],
        smem=[band_offsets],
        scratch=[pltpu.VMEM((3 * n_rows, leaf, BLK), F32)],
    )

    gathered = lax.all_to_all(skel.reshape(devices, share, rank), AXES, 0, 0)
    gathered = gathered.reshape(width, rank)
    if share % 8 == 0:
        (expand,) = staged(
            functools.partial(tree_kernel, share),
            [gathered, coupling, transfer],
            [((width, rank), F32)],
            mib=TREE_MIB,
        )
    else:
        expand = tree_plain(gathered, transfer, coupling, share)
    expand = lax.all_to_all(expand.reshape(devices, share, rank), AXES, 0, 0)
    expand = expand.reshape(width, rank)

    (total,) = staged(
        near_kernel,
        [order_perm, own_sum, near] + [rows for rows, _ in early],
        [((leaf, width), F32)],
    )
    (product,) = staged(
        last_kernel,
        [expand, far, left, total] + [rows for rows, _ in late],
        [((leaf, width), F32)],
        mib=LAST_MIB,
    )
    return product


def solution(mesh):
    split_rows = P(("gx", "gy"), None)
    placed = (split_rows,) * 4 + (P(("gx", "gy"), None, None, None), split_rows, P(), P())
    return jax.shard_map(body, mesh=mesh, in_specs=placed, out_specs=split_rows, check_vma=False)
```

time: 66.7 us -> 64.3 us (0.964)
  the two profiles are of different devices: /device:TPU:0 before, /device:TPU:1 now
where the time goes in v2:
time: 64.3 us; the launch traced here: 63.9 us
  starting transfers between devices  25.6 us (40%)
  Pallas kernels  19.3 us (30%)
  waiting for transfers between devices  17 us (26%)
  local copies, waits for them, and re-layouts  1.93 us (3%)
    pallas_call x4, Pallas kernels, staged(): pl.pallas_call(kernel, out_shape=[jax.ShapeDtypeStruct(shape, dtype) for...  16 us
    ppermute x3, waiting for transfers between devices, body(): fwd = lax.ppermute(sib, AXES, forward)  9.62 us
    ppermute x3, starting transfers between devices, body(): fwd = lax.ppermute(sib, AXES, forward)  9.32 us
    all_to_all x1, starting transfers between devices, body(): expand = lax.all_to_all(expand.reshape(devices, share, rank), AXES, 0, 0)  7.07 us
    ppermute x3, waiting for transfers between devices, body(): sib = lax.ppermute(own[c], AXES, sibling)  6.53 us
    all_to_all x1, starting transfers between devices, body(): gathered = lax.all_to_all(skel.reshape(devices, share, rank), AXES, 0, 0)  5.62 us
    ppermute x3, starting transfers between devices, body(): sib = lax.ppermute(own[c], AXES, sibling)  3.57 us
    pallas_call x1, Pallas kernels, body(): pl.pallas_call(first_kernel, out_shape=[jax.ShapeDtypeStruct((width, rank...  3.31 us
  transfers between devices with their start and end apart: 8, of which 4 were waited for; matrix products, arithmetic and copies ran while one was open for 0% of the time, Pallas kernels for 22%

profile of v2, /device:TPU:1, one launch (start us, length us, event | category | flops | bytes accessed | tf_op | source)
XLA Modules:
  0.0 63.9 jit_solution(10114089014812249815)
XLA Ops:
  0.0 3.3 %first.1 = (f32[512,128]{1,0:T(8,128)}, f32[128,512]{1,0:T(8,128)}, f32[128,512]{1,0:T(8,128)}, f32[256,512]{1,0:T(8,128)}) custom-call(s32[1,512]{1,0:T(1,128)} %refs_0_.3, f32[512,512]{1,0:T(8,128)} %x_ref.1, f32[512,128]{1,0:T(8,128)} %basis_ref.1), custom_call_target="tpu_custom_call" | custom-call | tf_op jit(solution)/shard_map/first/pallas_call | solution.py:290
  3.3 2.0 %collective-permute-start.4 = (f32[256,512]{1,0:T(8,128)}, f32[256,512]{1,0:T(8,128)S(1)}, u32[]{:S(2)}, u32[]{:S(2)}) collective-permute-start(f32[256,512]{1,0:T(8,128)} %get-tuple-element.16.refs_6_), channel_id=1, source_target_pairs={{0,1},{1,0},{2,3},{3,2},{4,5},{5,4},{6,7},{7,6},{8,9},{9,8},{10,11... | collective-permute-start | bytes 1572872 | tf_op jit(solution)/shard_map/ppermute | solution.py:302
  5.4 5.6 %all-to-all-start = ((f32[32,16,128]{2,1,0:T(8,128)}), f32[32,16,128]{2,1,0:T(8,128)S(1)}, u32[]{:S(2)}, u32[]{:S(2)}) async-start(f32[32,16,128]{2,1,0:T(8,128)} %bitcast.6), calls=%async_computation | async-start | bytes 524288 | tf_op jit(solution)/shard_map/all_to_all | solution.py:329
  11.0 1.4 %collective-permute-start = (f32[128,512]{1,0:T(8,128)}, f32[128,512]{1,0:T(8,128)S(1)}, u32[]{:S(2)}, u32[]{:S(2)}) collective-permute-start(f32[128,512]{1,0:T(8,128)} %get-tuple-element.14.refs_4_), channel_id=1, source_target_pairs={{0,1},{1,0},{2,3},{3,2},{4,5},{5,4},{6,7},{7,6},{8,9},{9,8},{10,11... | collective-permute-start | bytes 786440 | tf_op jit(solution)/shard_map/ppermute | solution.py:302
  12.4 0.1 collective-permute-start.2
  12.5 6.5 %collective-permute-done.4.refs_7_ = f32[256,512]{1,0:T(8,128)S(1)} collective-permute-done((f32[256,512]{1,0:T(8,128)}, f32[256,512]{1,0:T(8,128)S(1)}, u32[]{:S(2)}, u32[]{:S(2)}) %collective-permute-start.4) | collective-permute-done | bytes 524320 | tf_op jit(solution)/shard_map/ppermute | solution.py:302
  19.0 3.0 %collective-permute-start.5 = (f32[256,512]{1,0:T(8,128)S(1)}, f32[256,512]{1,0:T(8,128)S(1)}, u32[]{:S(2)}, u32[]{:S(2)}) collective-permute-start(f32[256,512]{1,0:T(8,128)S(1)} %collective-permute-done.4.refs_7_), channel_id=1, source_target_pairs={{0,2},{2,4},{3,1},{4,6},{5,3},{6,8},{7,5},{8,10},{9,7},{10,12},{11... | collective-permute-start | bytes 1572872 | tf_op jit(solution)/shard_map/ppermute | solution.py:306
  22.0 0.8 %all-to-all-done = f32[32,16,128]{2,1,0:T(8,128)S(1)} async-done(((f32[32,16,128]{2,1,0:T(8,128)}), f32[32,16,128]{2,1,0:T(8,128)S(1)}, u32[]{:S(2)}, u32[]{:S(2)}) %all-to-all-start) | async-done | bytes 262176 | tf_op jit(solution)/shard_map/all_to_all | solution.py:329
  22.8 0.0 copy-done.3
  22.8 0.0 copy-done.2
  22.8 3.0 %shard_map.82 = f32[512,128]{1,0:T(8,128)} custom-call(f32[512,128]{1,0:T(8,128)S(1)} %bitcast.5, f32[5,128,128]{2,1,0:T(8,128)S(1)} %copy-done.3, f32[4,2,128,128]{3,2,1,0:T(8,128)S(1)} %copy-done.2), custom_call_target="tpu_custom_call" | custom-call | tf_op jit(solution)/shard_map/pallas_call | solution.py:127
  25.8 7.1 %all-to-all-start.1 = ((f32[32,16,128]{2,1,0:T(8,128)}), f32[32,16,128]{2,1,0:T(8,128)S(1)}, u32[]{:S(2)}, u32[]{:S(2)}) async-start(f32[32,16,128]{2,1,0:T(8,128)} %bitcast.2), calls=%async_computation.1 | async-start | bytes 524288 | tf_op jit(solution)/shard_map/all_to_all | solution.py:340
  32.9 0.0 collective-permute-done.refs_3_
  32.9 0.0 copy-start.6
  32.9 3.3 %collective-permute-start.1 = (f32[128,512]{1,0:T(8,128)S(1)}, f32[128,512]{1,0:T(8,128)S(1)}, u32[]{:S(2)}, u32[]{:S(2)}) collective-permute-start(f32[128,512]{1,0:T(8,128)S(1)} %collective-permute-done.refs_3_), channel_id=1, source_target_pairs={{0,2},{2,4},{3,1},{4,6},{5,3},{6,8},{7,5},{8,10},{9,7},{10,12},{11... | collective-permute-start | bytes 786440 | tf_op jit(solution)/shard_map/ppermute | solution.py:306
  36.2 0.0 collective-permute-done.2.refs_5_
  36.2 0.0 copy-start.7
  36.2 3.1 %collective-permute-start.3 = (f32[128,512]{1,0:T(8,128)S(1)}, f32[128,512]{1,0:T(8,128)S(1)}, u32[]{:S(2)}, u32[]{:S(2)}) collective-permute-start(f32[128,512]{1,0:T(8,128)S(1)} %collective-permute-done.2.refs_5_), channel_id=1, source_target_pairs={{0,2},{2,4},{3,1},{4,6},{5,3},{6,8},{7,5},{8,10},{9,7},{10,12},{11... | collective-permute-start | bytes 786440 | tf_op jit(solution)/shard_map/ppermute | solution.py:306
  39.3 5.5 %shard_map.83 = (f32[512,512]{1,0:T(8,128)}, bf16[2,512,768]{2,1,0:T(8,128)(2,1)}, bf16[2,512,256]{2,1,0:T(8,128)(2,1)}, bf16[2,512,128]{2,1,0:T(8,128)(2,1)}) custom-call(s32[4,5]{1,0:T(4,128)} %refs_0_.2, f32[4,5,128,128]{3,2,1,0:T(8,128)} %refs_1_.3, s32[1,512]{1,0:T(1,128)} %refs_0_.3, f32[512,128]{1,0:T(8,128)} %refs_3_.1, ...), custom_call_target="tpu_custom_call" | custom-call | tf_op jit(solution)/shard_map/pallas_call | solution.py:127
  44.8 0.0 copy-done.5
  44.8 4.0 %collective-permute-done.1.refs_4_ = f32[128,512]{1,0:T(8,128)S(1)} collective-permute-done((f32[128,512]{1,0:T(8,128)S(1)}, f32[128,512]{1,0:T(8,128)S(1)}, u32[]{:S(2)}, u32[]{:S(2)}) %collective-permute-start.1) | collective-permute-done | bytes 262176 | tf_op jit(solution)/shard_map/ppermute | solution.py:306
  48.8 5.6 %collective-permute-done.3.refs_6_ = f32[128,512]{1,0:T(8,128)S(1)} collective-permute-done((f32[128,512]{1,0:T(8,128)S(1)}, f32[128,512]{1,0:T(8,128)S(1)}, u32[]{:S(2)}, u32[]{:S(2)}) %collective-permute-start.3) | collective-permute-done | bytes 262176 | tf_op jit(solution)/shard_map/ppermute | solution.py:306
  54.4 0.0 copy-done.8
  54.5 0.7 %copy-done.9 = f32[128,512]{1,0:T(8,128)} copy-done((f32[128,512]{1,0:T(8,128)}, f32[128,512]{1,0:T(8,128)S(1)}, u32[]{:S(2)}) %copy-start.9) | copy-done | bytes 262168
  55.1 5.4 %shard_map.84.refs_3_ = f32[512,512]{1,0:T(8,128)} custom-call(s32[1,512]{1,0:T(1,128)} %refs_0_.3, f32[512,512]{1,0:T(8,128)} %get-tuple-element.19.refs_1_, bf16[2,512,768]{2,1,0:T(8,128)(2,1)} %get-tuple-element.20.refs_2_, f32[128,512]{1,0:T(8,128)} %copy-done.6, f32[128,512]{1,0:T(8,128)} %copy-done.8, f32[128,512]{1,0:T(8,128)} %copy-done.7, ...), custom_call_target="tpu_custom_call" | custom-call | tf_op jit(solution)/shard_map/pallas_call | solution.py:127
  60.6 0.0 all-to-all-done.1
  60.6 0.0 collective-permute-done.5.refs_4_
  60.6 0.0 copy-done.1
  60.6 0.0 copy-done.4
  60.6 0.0 copy-start
  60.6 1.2 %copy-done = f32[512,512]{1,0:T(8,128)S(1)} copy-done((f32[512,512]{1,0:T(8,128)S(1)}, f32[512,512]{1,0:T(8,128)}, u32[]{:S(2)}) %copy-start) | copy-done | bytes 1048600
  61.9 2.1 %shard_map.85 = f32[512,512]{1,0:T(8,128)} custom-call(f32[512,128]{1,0:T(8,128)S(1)} %bitcast.4, bf16[2,512,128]{2,1,0:T(8,128)(2,1)S(1)} %copy-done.4, bf16[2,512,256]{2,1,0:T(8,128)(2,1)S(1)} %copy-done.1, f32[512,512]{1,0:T(8,128)S(1)} %copy-done, f32[256,512]{1,0:T(8,128)S(1)} %collective-permute-done.5.refs_4_), custom_call_target="tpu_custom_call" | custom-call | tf_op jit(solution)/shard_map/pallas_call | solution.py:127
  (9 shorter events, 0.0 us)
Async XLA Ops:
  0.0 22.8 %copy-start.3 = (f32[5,128,128]{2,1,0:T(8,128)S(1)}, f32[5,128,128]{2,1,0:T(8,128)}, u32[]{:S(2)}) copy-start(f32[5,128,128]{2,1,0:T(8,128)} %refs_1_.2) | copy-start | bytes 983044
  0.0 22.8 %copy-start.2 = (f32[4,2,128,128]{3,2,1,0:T(8,128)S(1)}, f32[4,2,128,128]{3,2,1,0:T(8,128)}, u32[]{:S(2)}) copy-start(f32[4,2,128,128]{3,2,1,0:T(8,128)} %refs_2_.2) | copy-start | bytes 1572868
  3.3 15.7 %collective-permute-start.4 = (f32[256,512]{1,0:T(8,128)}, f32[256,512]{1,0:T(8,128)S(1)}, u32[]{:S(2)}, u32[]{:S(2)}) collective-permute-start(f32[256,512]{1,0:T(8,128)} %get-tuple-element.16.refs_6_), channel_id=1, source_target_pairs={{0,1},{1,0},{2,3},{3,2},{4,5},{5,4},{6,7},{7,6},{8,9},{9,8},{10,11... | collective-permute-start | bytes 1572872 | tf_op jit(solution)/shard_map/ppermute | solution.py:302
  5.4 17.5 %all-to-all-start = ((f32[32,16,128]{2,1,0:T(8,128)}), f32[32,16,128]{2,1,0:T(8,128)S(1)}, u32[]{:S(2)}, u32[]{:S(2)}) async-start(f32[32,16,128]{2,1,0:T(8,128)} %bitcast.6), calls=%async_computation | async-start | bytes 524288 | tf_op jit(solution)/shard_map/all_to_all | solution.py:329
  11.0 21.9 %collective-permute-start = (f32[128,512]{1,0:T(8,128)}, f32[128,512]{1,0:T(8,128)S(1)}, u32[]{:S(2)}, u32[]{:S(2)}) collective-permute-start(f32[128,512]{1,0:T(8,128)} %get-tuple-element.14.refs_4_), channel_id=1, source_target_pairs={{0,1},{1,0},{2,3},{3,2},{4,5},{5,4},{6,7},{7,6},{8,9},{9,8},{10,11... | collective-permute-start | bytes 786440 | tf_op jit(solution)/shard_map/ppermute | solution.py:302
  12.4 23.8 %collective-permute-start.2 = (f32[128,512]{1,0:T(8,128)}, f32[128,512]{1,0:T(8,128)S(1)}, u32[]{:S(2)}, u32[]{:S(2)}) collective-permute-start(f32[128,512]{1,0:T(8,128)} %get-tuple-element.15.refs_5_), channel_id=1, source_target_pairs={{0,1},{1,0},{2,3},{3,2},{4,5},{5,4},{6,7},{7,6},{8,9},{9,8},{10,11... | collective-permute-start | bytes 786440 | tf_op jit(solution)/shard_map/ppermute | solution.py:302
  19.0 25.8 %copy-start.5 = (f32[256,512]{1,0:T(8,128)}, f32[256,512]{1,0:T(8,128)S(1)}, u32[]{:S(2)}) copy-start(f32[256,512]{1,0:T(8,128)S(1)} %collective-permute-done.4.refs_7_) | copy-start | bytes 1572868
  19.0 41.6 %collective-permute-start.5 = (f32[256,512]{1,0:T(8,128)S(1)}, f32[256,512]{1,0:T(8,128)S(1)}, u32[]{:S(2)}, u32[]{:S(2)}) collective-permute-start(f32[256,512]{1,0:T(8,128)S(1)} %collective-permute-done.4.refs_7_), channel_id=1, source_target_pairs={{0,2},{2,4},{3,1},{4,6},{5,3},{6,8},{7,5},{8,10},{9,7},{10,12},{11... | collective-permute-start | bytes 1572872 | tf_op jit(solution)/shard_map/ppermute | solution.py:306
  25.8 34.8 %all-to-all-start.1 = ((f32[32,16,128]{2,1,0:T(8,128)}), f32[32,16,128]{2,1,0:T(8,128)S(1)}, u32[]{:S(2)}, u32[]{:S(2)}) async-start(f32[32,16,128]{2,1,0:T(8,128)} %bitcast.2), calls=%async_computation.1 | async-start | bytes 524288 | tf_op jit(solution)/shard_map/all_to_all | solution.py:340
  32.9 21.5 %copy-start.6 = (f32[128,512]{1,0:T(8,128)}, f32[128,512]{1,0:T(8,128)S(1)}, u32[]{:S(2)}) copy-start(f32[128,512]{1,0:T(8,128)S(1)} %collective-permute-done.refs_3_) | copy-start | bytes 786436
  32.9 15.9 %collective-permute-start.1 = (f32[128,512]{1,0:T(8,128)S(1)}, f32[128,512]{1,0:T(8,128)S(1)}, u32[]{:S(2)}, u32[]{:S(2)}) collective-permute-start(f32[128,512]{1,0:T(8,128)S(1)} %collective-permute-done.refs_3_), channel_id=1, source_target_pairs={{0,2},{2,4},{3,1},{4,6},{5,3},{6,8},{7,5},{8,10},{9,7},{10,12},{11... | collective-permute-start | bytes 786440 | tf_op jit(solution)/shard_map/ppermute | solution.py:306
  36.2 18.2 %copy-start.7 = (f32[128,512]{1,0:T(8,128)}, f32[128,512]{1,0:T(8,128)S(1)}, u32[]{:S(2)}) copy-start(f32[128,512]{1,0:T(8,128)S(1)} %collective-permute-done.2.refs_5_) | copy-start | bytes 786436
  36.2 18.2 %collective-permute-start.3 = (f32[128,512]{1,0:T(8,128)S(1)}, f32[128,512]{1,0:T(8,128)S(1)}, u32[]{:S(2)}, u32[]{:S(2)}) collective-permute-start(f32[128,512]{1,0:T(8,128)S(1)} %collective-permute-done.2.refs_5_), channel_id=1, source_target_pairs={{0,2},{2,4},{3,1},{4,6},{5,3},{6,8},{7,5},{8,10},{9,7},{10,12},{11... | collective-permute-start | bytes 786440 | tf_op jit(solution)/shard_map/ppermute | solution.py:306
  48.8 5.6 %copy-start.8 = (f32[128,512]{1,0:T(8,128)}, f32[128,512]{1,0:T(8,128)S(1)}, u32[]{:S(2)}) copy-start(f32[128,512]{1,0:T(8,128)S(1)} %collective-permute-done.1.refs_4_) | copy-start | bytes 786436
  54.4 0.7 %copy-start.9 = (f32[128,512]{1,0:T(8,128)}, f32[128,512]{1,0:T(8,128)S(1)}, u32[]{:S(2)}) copy-start(f32[128,512]{1,0:T(8,128)S(1)} %collective-permute-done.3.refs_6_) | copy-start | bytes 786436
  55.1 5.5 %copy-start.1 = (bf16[2,512,256]{2,1,0:T(8,128)(2,1)S(1)}, bf16[2,512,256]{2,1,0:T(8,128)(2,1)}, u32[]{:S(2)}) copy-start(bf16[2,512,256]{2,1,0:T(8,128)(2,1)} %get-tuple-element.18.refs_2_) | copy-start | bytes 1572868
  55.1 5.5 %copy-start.4 = (bf16[2,512,128]{2,1,0:T(8,128)(2,1)S(1)}, bf16[2,512,128]{2,1,0:T(8,128)(2,1)}, u32[]{:S(2)}) copy-start(bf16[2,512,128]{2,1,0:T(8,128)(2,1)} %get-tuple-element.17.refs_1_) | copy-start | bytes 786436
  60.6 1.2 %copy-start = (f32[512,512]{1,0:T(8,128)S(1)}, f32[512,512]{1,0:T(8,128)}, u32[]{:S(2)}) copy-start(f32[512,512]{1,0:T(8,128)} %shard_map.84.refs_3_) | copy-start | bytes 3145732
